TPU v7x, 32 devices: a whole 2x2x4 slice. The times are simulated.
32 devices in a mesh: expert: 8 (over z, x), fsdp: 4 (over y, core).
Axes of the slice: x: 2, y: 2, z: 4, core: 2. Of those that a mesh axis runs over, the one named last changes fastest.
Arguments:
- tokens: bfloat16 [160, 197, 512], P(('expert', 'fsdp')), may hold values from -6 to 6
- ln1_gain: bfloat16 [512], P('fsdp'), may hold values from 0.5 to 1.5
- ln1_bias: bfloat16 [512], P('fsdp'), may hold values from -1.796875 to 1.796875
- w_qkv: bfloat16 [512, 1536], P('fsdp'), may hold values from -0.25 to 0.25
- q_bias: bfloat16 [512], P('fsdp'), may hold values from -1.796875 to 1.796875
- v_bias: bfloat16 [512], P('fsdp'), may hold values from -1.796875 to 1.796875
- w_out: bfloat16 [512, 512], P('fsdp'), may hold values from -1.5 to 1.5
- out_bias: bfloat16 [512], P('fsdp'), may hold values from -1.796875 to 1.796875
- ln2_gain: bfloat16 [512], P('fsdp'), may hold values from 0.5 to 1.5
- ln2_bias: bfloat16 [512], P('fsdp'), may hold values from -1.796875 to 1.796875
- w_router: bfloat16 [512, 8], P('fsdp'), may hold values from -0.1875 to 0.1875
- expert_w1: bfloat16 [8, 512, 2048], P('expert', 'fsdp'), may hold values from -0.25 to 0.25
- expert_b1: bfloat16 [8, 2048], P('expert', 'fsdp'), may hold values from -1.796875 to 1.796875
- expert_w2: bfloat16 [8, 2048, 512], P('expert', 'fsdp'), may hold values from -0.75 to 0.75
- expert_b2: bfloat16 [8, 512], P('expert', 'fsdp'), may hold values from -6 to 6
- route_ids: int32 [31520, 2], P(('expert', 'fsdp')), may hold values from 0 to 7, all different within a row; in each aligned block of 985 rows (0 to 984, 985 to 1969, ...) at most 432 rows name the same one
- clip_threshold: int32 [8], replicated, may hold values from 2 to 4
- grad_output: bfloat16 [160, 197, 512], P(('expert', 'fsdp')), may hold values from -6 to 6
Outputs:
- output: bfloat16 [160, 197, 512], P(('expert', 'fsdp'))
- input_grad: float32 [160, 197, 512], P(('expert', 'fsdp'))
- grad_ln1_gain: float32 [512], P('fsdp')
- grad_ln1_bias: float32 [512], P('fsdp')
- grad_w_qkv: float32 [512, 1536], P('fsdp')
- grad_q_bias: float32 [512], P('fsdp')
- grad_v_bias: float32 [512], P('fsdp')
- grad_w_out: float32 [512, 512], P('fsdp')
- grad_out_bias: float32 [512], P('fsdp')
- grad_ln2_gain: float32 [512], P('fsdp')
- grad_ln2_bias: float32 [512], P('fsdp')
- grad_w_router: float32 [512, 8], P('fsdp')
- grad_expert_w1: float32 [8, 512, 2048], P('expert', 'fsdp')
- grad_expert_b1: float32 [8, 2048], P('expert', 'fsdp')
- grad_expert_w2: float32 [8, 2048, 512], P('expert', 'fsdp')
- grad_expert_b2: float32 [8, 512], P('expert', 'fsdp')
- clipped_qkv: bfloat16 [512, 1536], P('fsdp')
Inputs may be any that keep to these rules, and one draw needn't show every extreme that they name: `route_ids`: each row names 2 different experts; among the 985 rows of one device no expert is named by more than 432 rows, and in some device's rows one expert is named by exactly 432.
All inputs are finite; a program needn't handle non-finite values.
Results may differ from a plain program's by a relative error of at most 0.024.
Values may be sent and summed in bfloat16 or wider, within the bound.
No kernel may reach another device: no remote copies, remote signals or barrier semaphores. Data moves between devices by JAX's collectives and lax.ppermute only.
A program may use at most 256 MiB of HBM per device.

v0:
```python
import jax
import jax.numpy as jnp
from jax import lax
from jax.sharding import PartitionSpec as P

HEADS = 8
norm_eps = 1e-06
highest = lax.Precision.HIGHEST


def layer_norm(matrix, norm_gain, norm_shift):
    centred = matrix - jnp.mean(matrix, axis=1, keepdims=True)
    inverse = lax.rsqrt(jnp.mean(centred * centred, axis=1, keepdims=True) + norm_eps)
    normed = centred * inverse
    return (normed * norm_gain + norm_shift, normed, inverse)


def norm_backward(upstream, norm_gain, normed, inverse):
    scaled = upstream * norm_gain
    spread = (
        scaled
        - jnp.mean(scaled, axis=1, keepdims=True)
        - normed * jnp.mean(scaled * normed, axis=1, keepdims=True)
    )
    return (spread * inverse, jnp.sum(upstream * normed, axis=0), jnp.sum(upstream, axis=0))


def gelu_exact(values):
    return jax.nn.gelu(values, approximate=False)


def shards(
    tokens,
    ln1_gain,
    ln1_bias,
    w_qkv,
    q_bias,
    v_bias,
    w_out,
    out_bias,
    ln2_gain,
    ln2_bias,
    w_router,
    expert_w1,
    expert_b1,
    expert_w2,
    expert_b2,
    route_ids,
    clip_threshold,
    grad_output,
):
    gathered = (
        lax.all_gather(ln1_gain, "fsdp", axis=0, tiled=True),
        lax.all_gather(ln1_bias, "fsdp", axis=0, tiled=True),
        lax.all_gather(w_qkv, "fsdp", axis=0, tiled=True),
        lax.all_gather(q_bias, "fsdp", axis=0, tiled=True),
        lax.all_gather(v_bias, "fsdp", axis=0, tiled=True),
        lax.all_gather(w_out, "fsdp", axis=0, tiled=True),
        lax.all_gather(out_bias, "fsdp", axis=0, tiled=True),
        lax.all_gather(ln2_gain, "fsdp", axis=0, tiled=True),
        lax.all_gather(ln2_bias, "fsdp", axis=0, tiled=True),
        lax.all_gather(w_router, "fsdp", axis=0, tiled=True),
        lax.all_gather(expert_w1, "fsdp", axis=1, tiled=True),
        lax.all_gather(expert_b1, "fsdp", axis=1, tiled=True),
        lax.all_gather(expert_w2, "fsdp", axis=1, tiled=True),
        lax.all_gather(expert_b2, "fsdp", axis=1, tiled=True),
    )
    gain_one = gathered[0].astype(jnp.float32)
    shift_one = gathered[1].astype(jnp.float32)
    qkv_weight = gathered[2]
    query_bias = gathered[3].astype(jnp.float32)
    value_bias = gathered[4].astype(jnp.float32)
    out_weight = gathered[5]
    out_shift = gathered[6].astype(jnp.float32)
    gain_two = gathered[7].astype(jnp.float32)
    shift_two = gathered[8].astype(jnp.float32)
    router_weight = gathered[9].astype(jnp.float32)
    first_weight = gathered[10][0]
    first_bias = gathered[11][0].astype(jnp.float32)
    second_weight = gathered[12][0]
    second_bias = gathered[13][0].astype(jnp.float32)
    image_count, sequence, feature_width = tokens.shape
    token_count = image_count * sequence
    head_count = HEADS
    head_size = feature_width // head_count
    score_scale = head_size ** (-0.5)
    route_top = route_ids.shape[1]
    expert_total = router_weight.shape[1]
    capacity = (7 * token_count // (2 * expert_total) + 7) // 8 * 8
    head_shape = (image_count, sequence, head_count, head_size)
    residual = tokens.astype(jnp.float32).reshape(token_count, feature_width)
    normed_in, hat_one, inverse_one = layer_norm(residual, gain_one, shift_one)
    normed_low = normed_in.astype(jnp.bfloat16)
    projected = jnp.dot(normed_low, qkv_weight, preferred_element_type=jnp.float32)
    queries = (projected[:, :feature_width] + query_bias).astype(jnp.bfloat16).reshape(head_shape)
    key_rows = (
        projected[:, feature_width : 2 * feature_width].astype(jnp.bfloat16).reshape(head_shape)
    )
    value_rows = (
        (projected[:, 2 * feature_width :] + value_bias).astype(jnp.bfloat16).reshape(head_shape)
    )
    scores = (
        jnp.einsum("bqhd,bkhd->bhqk", queries, key_rows, preferred_element_type=jnp.float32)
        * score_scale
    )
    head_peak = jnp.max(scores, axis=(0, 2, 3))
    row_top = jnp.max(scores, axis=3, keepdims=True)
    log_total = row_top + jnp.log(jnp.sum(jnp.exp(scores - row_top), axis=3, keepdims=True))
    attn_low = jnp.exp(scores - log_total).astype(jnp.bfloat16)
    mixed_rows = jnp.einsum(
        "bhqk,bkhd->bqhd", attn_low, value_rows, preferred_element_type=jnp.float32
    )
    mixed_low = mixed_rows.astype(jnp.bfloat16).reshape(token_count, feature_width)
    hidden = (
        residual + jnp.dot(mixed_low, out_weight, preferred_element_type=jnp.float32) + out_shift
    )
    normed_mid, hat_two, inverse_two = layer_norm(hidden, gain_two, shift_two)
    route_prob = jax.nn.softmax(jnp.dot(normed_mid, router_weight, precision=highest), axis=1)
    picked = (
        route_ids[:, :, None] == lax.broadcasted_iota(jnp.int32, (1, 1, expert_total), 2)
    ).astype(jnp.int32)
    picked_float = picked.astype(jnp.float32)
    gate_values = jnp.sum(picked_float * route_prob[:, None, :], axis=2)
    picked_flat = picked.reshape(token_count * route_top, expert_total)
    slot_rank = jnp.sum(
        (jnp.cumsum(picked_flat, axis=0, dtype=jnp.int32) - picked_flat) * picked_flat,
        axis=1,
        dtype=jnp.int32,
    )
    slot_index = route_ids.reshape(-1) * capacity + slot_rank
    mid_low = normed_mid.astype(jnp.bfloat16)
    slot_rows = jnp.broadcast_to(
        mid_low[:, None, :], (token_count, route_top, feature_width)
    ).reshape(token_count * route_top, feature_width)
    outgoing = (
        jnp.zeros((expert_total * capacity, feature_width), jnp.bfloat16)
        .at[slot_index]
        .set(slot_rows)
        .reshape(expert_total, capacity, feature_width)
    )
    arrived = lax.all_to_all(outgoing, "expert", split_axis=0, concat_axis=0, tiled=True)
    flat_in = arrived.reshape(-1, feature_width)
    activation = gelu_exact(
        jnp.dot(flat_in, first_weight, preferred_element_type=jnp.float32) + first_bias
    ).astype(jnp.bfloat16)
    result = (
        jnp.dot(activation, second_weight, preferred_element_type=jnp.float32) + second_bias
    ).astype(jnp.bfloat16)
    produced = result.reshape(arrived.shape)
    returned = lax.all_to_all(produced, "expert", split_axis=0, concat_axis=0, tiled=True)
    slot_out = (
        returned.reshape(expert_total * capacity, feature_width)[slot_index]
        .astype(jnp.float32)
        .reshape(token_count, route_top, feature_width)
    )
    output = (
        (hidden + jnp.sum(gate_values[:, :, None] * slot_out, axis=1))
        .astype(jnp.bfloat16)
        .reshape(tokens.shape)
    )
    upstream = grad_output.astype(jnp.float32).reshape(token_count, feature_width)
    gate_grad = jnp.sum(slot_out * upstream[:, None, :], axis=2)
    slot_grad = (
        (gate_values[:, :, None] * upstream[:, None, :])
        .astype(jnp.bfloat16)
        .reshape(token_count * route_top, feature_width)
    )
    grad_buffer = (
        jnp.zeros((expert_total * capacity, feature_width), jnp.bfloat16)
        .at[slot_index]
        .set(slot_grad)
        .reshape(expert_total, capacity, feature_width)
    )
    grad_arrived = lax.all_to_all(grad_buffer, "expert", split_axis=0, concat_axis=0, tiled=True)
    flat_rows = arrived.reshape(-1, feature_width)
    flat_grad = grad_arrived.reshape(-1, feature_width)
    activation, gelu_back = jax.vjp(
        gelu_exact,
        jnp.dot(flat_rows, first_weight, preferred_element_type=jnp.float32) + first_bias,
    )
    act_low = activation.astype(jnp.bfloat16)
    grad_second = jnp.einsum("rh,rd->hd", act_low, flat_grad, preferred_element_type=jnp.float32)
    grad_second_bias = jnp.sum(flat_grad, axis=0, dtype=jnp.float32)
    act_grad = jnp.einsum("rd,hd->rh", flat_grad, second_weight, preferred_element_type=jnp.float32)
    pre_grad = gelu_back(act_grad)[0].astype(jnp.bfloat16)
    grad_first = jnp.einsum("rd,rh->dh", flat_rows, pre_grad, preferred_element_type=jnp.float32)
    grad_first_bias = jnp.sum(pre_grad, axis=0, dtype=jnp.float32)
    row_grad = (
        jnp.einsum("rh,dh->rd", pre_grad, first_weight, preferred_element_type=jnp.float32)
        .astype(jnp.bfloat16)
        .reshape(grad_arrived.shape)
    )
    row_back = lax.all_to_all(row_grad, "expert", split_axis=0, concat_axis=0, tiled=True)
    slot_back = (
        row_back.reshape(expert_total * capacity, feature_width)[slot_index]
        .astype(jnp.float32)
        .reshape(token_count, route_top, feature_width)
    )
    prob_grad = jnp.sum(picked_float * gate_grad[:, :, None], axis=1)
    logit_grad = route_prob * (prob_grad - jnp.sum(route_prob * prob_grad, axis=1, keepdims=True))
    mid_grad = jnp.sum(slot_back, axis=1) + jnp.einsum(
        "re,de->rd", logit_grad, router_weight, precision=highest
    )
    grad_router = jnp.einsum("rd,re->de", normed_mid, logit_grad, precision=highest)
    norm_part, grad_gain_two, grad_shift_two = norm_backward(
        mid_grad, gain_two, hat_two, inverse_two
    )
    hidden_grad = upstream + norm_part
    branch_low = hidden_grad.astype(jnp.bfloat16)
    grad_out_weight = jnp.einsum(
        "rd,re->de", mixed_low, branch_low, preferred_element_type=jnp.float32
    )
    grad_out_shift = jnp.sum(branch_low, axis=0, dtype=jnp.float32)
    mixed_grad = (
        jnp.einsum("re,de->rd", branch_low, out_weight, preferred_element_type=jnp.float32)
        .astype(jnp.bfloat16)
        .reshape(head_shape)
    )
    score_again = (
        jnp.einsum("bqhd,bkhd->bhqk", queries, key_rows, preferred_element_type=jnp.float32)
        * score_scale
    )
    attn_prob = jnp.exp(score_again - log_total)
    value_grad = jnp.einsum(
        "bhqk,bqhd->bkhd",
        attn_prob.astype(jnp.bfloat16),
        mixed_grad,
        preferred_element_type=jnp.float32,
    ).astype(jnp.bfloat16)
    weight_grad = jnp.einsum(
        "bqhd,bkhd->bhqk", mixed_grad, value_rows, preferred_element_type=jnp.float32
    )
    score_grad = (
        attn_prob * (weight_grad - jnp.sum(attn_prob * weight_grad, axis=3, keepdims=True))
    ).astype(jnp.bfloat16)
    query_grad = (
        jnp.einsum("bhqk,bkhd->bqhd", score_grad, key_rows, preferred_element_type=jnp.float32)
        * score_scale
    ).astype(jnp.bfloat16)
    key_grad = (
        jnp.einsum("bhqk,bqhd->bkhd", score_grad, queries, preferred_element_type=jnp.float32)
        * score_scale
    ).astype(jnp.bfloat16)
    qkv_grad = jnp.concatenate(
        [
            query_grad.reshape(token_count, feature_width),
            key_grad.reshape(token_count, feature_width),
            value_grad.reshape(token_count, feature_width),
        ],
        axis=1,
    )
    grad_qkv = jnp.einsum("rd,re->de", normed_low, qkv_grad, preferred_element_type=jnp.float32)
    grad_query_bias = jnp.sum(qkv_grad[:, :feature_width], axis=0, dtype=jnp.float32)
    grad_value_bias = jnp.sum(qkv_grad[:, 2 * feature_width :], axis=0, dtype=jnp.float32)
    in_grad = jnp.einsum("re,de->rd", qkv_grad, qkv_weight, preferred_element_type=jnp.float32)
    input_part, grad_gain_one, grad_shift_one = norm_backward(
        in_grad, gain_one, hat_one, inverse_one
    )
    input_grad = (hidden_grad + input_part).reshape(tokens.shape)
    shares = (
        lax.psum_scatter(
            grad_gain_one.astype(jnp.bfloat16), "fsdp", scatter_dimension=0, tiled=True
        ).astype(jnp.float32),
        lax.psum_scatter(
            grad_shift_one.astype(jnp.bfloat16), "fsdp", scatter_dimension=0, tiled=True
        ).astype(jnp.float32),
        lax.psum_scatter(
            grad_qkv.astype(jnp.bfloat16), "fsdp", scatter_dimension=0, tiled=True
        ).astype(jnp.float32),
        lax.psum_scatter(
            grad_query_bias.astype(jnp.bfloat16), "fsdp", scatter_dimension=0, tiled=True
        ).astype(jnp.float32),
        lax.psum_scatter(
            grad_value_bias.astype(jnp.bfloat16), "fsdp", scatter_dimension=0, tiled=True
        ).astype(jnp.float32),
        lax.psum_scatter(
            grad_out_weight.astype(jnp.bfloat16), "fsdp", scatter_dimension=0, tiled=True
        ).astype(jnp.float32),
        lax.psum_scatter(
            grad_out_shift.astype(jnp.bfloat16), "fsdp", scatter_dimension=0, tiled=True
        ).astype(jnp.float32),
        lax.psum_scatter(
            grad_gain_two.astype(jnp.bfloat16), "fsdp", scatter_dimension=0, tiled=True
        ).astype(jnp.float32),
        lax.psum_scatter(
            grad_shift_two.astype(jnp.bfloat16), "fsdp", scatter_dimension=0, tiled=True
        ).astype(jnp.float32),
        lax.psum_scatter(
            grad_router.astype(jnp.bfloat16), "fsdp", scatter_dimension=0, tiled=True
        ).astype(jnp.float32),
    )
    summed = (
        lax.psum(shares[0].astype(jnp.bfloat16), "expert").astype(jnp.float32),
        lax.psum(shares[1].astype(jnp.bfloat16), "expert").astype(jnp.float32),
        lax.psum(shares[2].astype(jnp.bfloat16), "expert").astype(jnp.float32),
        lax.psum(shares[3].astype(jnp.bfloat16), "expert").astype(jnp.float32),
        lax.psum(shares[4].astype(jnp.bfloat16), "expert").astype(jnp.float32),
        lax.psum(shares[5].astype(jnp.bfloat16), "expert").astype(jnp.float32),
        lax.psum(shares[6].astype(jnp.bfloat16), "expert").astype(jnp.float32),
        lax.psum(shares[7].astype(jnp.bfloat16), "expert").astype(jnp.float32),
        lax.psum(shares[8].astype(jnp.bfloat16), "expert").astype(jnp.float32),
        lax.psum(shares[9].astype(jnp.bfloat16), "expert").astype(jnp.float32),
    )
    expert_summed = (
        lax.psum_scatter(
            grad_first[None].astype(jnp.bfloat16), "fsdp", scatter_dimension=1, tiled=True
        ).astype(jnp.float32),
        lax.psum_scatter(
            grad_first_bias[None].astype(jnp.bfloat16), "fsdp", scatter_dimension=1, tiled=True
        ).astype(jnp.float32),
        lax.psum_scatter(
            grad_second[None].astype(jnp.bfloat16), "fsdp", scatter_dimension=1, tiled=True
        ).astype(jnp.float32),
        lax.psum_scatter(
            grad_second_bias[None].astype(jnp.bfloat16), "fsdp", scatter_dimension=1, tiled=True
        ).astype(jnp.float32),
    )
    peak_logit = lax.pmax(head_peak, ("expert", "fsdp"))
    limit_value = clip_threshold.astype(jnp.float32)
    root_factor = jnp.sqrt(limit_value / jnp.maximum(peak_logit, limit_value))
    column_scale = jnp.concatenate(
        [
            jnp.repeat(root_factor, head_size),
            jnp.repeat(root_factor, head_size),
            jnp.ones((feature_width,), jnp.float32),
        ]
    )
    clipped_qkv = (w_qkv.astype(jnp.float32) * column_scale).astype(jnp.bfloat16)
    return (
        output,
        input_grad,
        summed[0],
        summed[1],
        summed[2],
        summed[3],
        summed[4],
        summed[5],
        summed[6],
        summed[7],
        summed[8],
        summed[9],
        expert_summed[0],
        expert_summed[1],
        expert_summed[2],
        expert_summed[3],
        clipped_qkv,
    )


def solution(mesh):
    placed = (
        P(("expert", "fsdp"), None, None),
        P("fsdp"),
        P("fsdp"),
        P("fsdp", None),
        P("fsdp"),
        P("fsdp"),
        P("fsdp", None),
        P("fsdp"),
        P("fsdp"),
        P("fsdp"),
        P("fsdp", None),
        P("expert", "fsdp", None),
        P("expert", "fsdp"),
        P("expert", "fsdp", None),
        P("expert", "fsdp"),
        P(("expert", "fsdp"), None),
        P(),
        P(("expert", "fsdp"), None, None),
    )
    return jax.shard_map(
        shards,
        mesh=mesh,
        in_specs=placed,
        out_specs=(
            P(("expert", "fsdp"), None, None),
            P(("expert", "fsdp"), None, None),
            P("fsdp"),
            P("fsdp"),
            P("fsdp", None),
            P("fsdp"),
            P("fsdp"),
            P("fsdp", None),
            P("fsdp"),
            P("fsdp"),
            P("fsdp"),
            P("fsdp", None),
            P("expert", "fsdp", None),
            P("expert", "fsdp"),
            P("expert", "fsdp", None),
            P("expert", "fsdp"),
            P("fsdp", None),
        ),
        check_vma=False,
    )
```

profile of v0, /device:TPU:0, one launch (start us, length us, event | category | flops | bytes accessed | tf_op | source)
XLA Modules:
  0.0 718.8 jit_solution(18381751544721613083)
XLA Ops:
  11.8 6.0 all-gather
  17.8 5.3 all-gather.1
  23.1 5.0 all-gather.2
  28.2 5.0 all-gather.3
  33.2 5.0 all-gather.4
  38.2 5.0 all-gather.5
  43.3 5.0 all-gather.6
  52.3 7.9 %all_gather.47 = bf16[512,512]{1,0:T(8,128)(2,1)} all-gather(bf16[128,512]{1,0:T(8,128)(2,1)S(1)} %copy-done.46), channel_id=1, replica_groups=mesh['expert'=8,'fsdp'=4] {'fsdp'}, dimensions={0}, use_global_device_ids=true | all-gather | bytes 655360 | tf_op jit(solution)/shard_map/all_gather | solution.py:58
  60.2 3.2 fusion.44
  68.6 3.4 copy.109
  74.4 3.1 copy.110
  85.4 5.5 fusion.26
  90.9 2.7 copy.113
  93.5 3.1 reshape.282
  96.7 2.9 fusion.46
  102.7 5.6 reshape.330
  108.3 13.3 %scatter_custom_fusion = bf16[3456,512]{1,0:T(8,128)(2,1)} fusion(s32[1970]{0:T(1024)S(1)} %bitcast.131, bf16[1970,512]{1,0:T(8,128)(2,1)} %reshape.330, bf16[]{:T(256)} %constant.17.clone.1), kind=kCustom, calls=%fused_computation.69 | custom fusion | bytes 3539456 | tf_op jit(solution)/shard_map/scatter | solution.py:138
  121.6 6.0 all-to-all-start
  130.6 4.8 mul.251
  135.5 6.1 mul.252
  141.6 5.2 all_gather.53
  146.8 5.0 all_gather.55
  152.4 5.6 all_gather.51
  161.2 18.5 %scatter_custom_fusion.1 = bf16[3456,512]{1,0:T(8,128)(2,1)} fusion(s32[1970]{0:T(1024)S(1)} %bitcast.132, f32[1970,512]{1,0:T(8,128)} %mul.252, f32[1970]{0:T(1024)S(1)} %mul.249, bf16[]{:T(256)} %constant.17.clone.1), kind=kCustom, calls=%fused_computation.63 | custom fusion | flops 2017280 | bytes 7581698 | tf_op jit(solution)/shard_map/scatter | solution.py:171
  179.8 27.6 %all-to-all-done = bf16[8,432,512]{2,1,0:T(8,128)(2,1)} async-done(((bf16[8,432,512]{2,1,0:T(8,128)(2,1)}), bf16[8,432,512]{2,1,0:T(8,128)(2,1)}, u32[]{:S(2)}, u32[]{:S(2)}) %all-to-all-start) | async-done | bytes 3538976 | tf_op jit(solution)/shard_map/all_to_all | solution.py:141
  207.3 4.7 all-to-all-start.2
  212.0 70.8 %multiply_convert_fusion = (bf16[3456,2048]{1,0:T(8,128)(2,1)}, f32[3456,2048]{1,0:T(8,128)}, f32[3456,2048]{1,0:T(8,128)}) fusion(f32[2048]{0:T(1024)S(1)} %bitcast.142, bf16[3456,512]{1,0:T(8,128)(2,1)} %bitcast.19, bf16[1,512,2048]{2,1,0:T(8,128)(2,1)} %all-gather.13.cloned.1.call-done), kind=kOutput, calls=%fused_computation.7 | convolution fusion | flops 7714897920 | bytes 76423168 | tf_op jit(solution)/shard_map/dot_general | solution.py:144
  282.8 12.5 %add_convert_fusion.1 = bf16[3456,512]{1,0:T(8,128)(2,1)} fusion(bf16[3456,2048]{1,0:T(8,128)(2,1)} %get-tuple-element.48, f32[512]{0:T(512)S(1)} %bitcast.144, bf16[1,2048,512]{2,1,0:T(8,128)(2,1)} %all-gather.15.cloned.1.call-done), kind=kOutput, calls=%fused_computation.25 | convolution fusion | flops 7251296256 | bytes 19793920 | tf_op jit(solution)/shard_map/dot_general | solution.py:147
  295.4 6.0 all-to-all-start.1
  305.0 31.9 %fusion.50 = (bf16[2048]{0:T(1024)(128)(2,1)S(1)}, bf16[3456,2048]{1,0:T(8,128)(2,1)}) fusion(f32[3456,2048]{1,0:T(8,128)} %get-tuple-element.49, bf16[3456,512]{1,0:T(8,128)(2,1)} %bitcast.27, bf16[1,2048,512]{2,1,0:T(8,128)(2,1)} %all-gather.15.cloned.1.call-done, f32[3456,2048]{1,0:T(8,128)} %get-tuple-element.57, f32[2048]{0:T(1024)S(1)} %bitcast.143), kind=kOutput, calls=%fused_computation.138 | convolution fusion | flops 7361001472 | bytes 76427264 | tf_op jit(solution)/shard_map/rd,hd->rh/dot_general | solution.py:184
  338.1 12.6 %convolution_convert_fusion = bf16[3456,512]{1,0:T(8,128)(2,1)} fusion(bf16[3456,2048]{1,0:T(8,128)(2,1)} %get-tuple-element.68, bf16[1,512,2048]{2,1,0:T(8,128)(2,1)} %all-gather.13.cloned.1.call-done), kind=kOutput, calls=%fused_computation.28 | convolution fusion | flops 7249526784 | bytes 19791872 | tf_op jit(solution)/shard_map/rh,dh->rd/dot_general | solution.py:189
  350.7 28.8 %all-to-all-done.1 = bf16[8,432,512]{2,1,0:T(8,128)(2,1)S(1)} async-done(((bf16[8,432,512]{2,1,0:T(8,128)(2,1)}), bf16[8,432,512]{2,1,0:T(8,128)(2,1)S(1)}, u32[]{:S(2)}, u32[]{:S(2)}) %all-to-all-start.1) | async-done | bytes 3538976 | tf_op jit(solution)/shard_map/all_to_all | solution.py:150
  379.6 4.5 all-to-all-start.3
  384.1 13.0 %fusion.7 = bf16[1,2048,512]{2,1,0:T(8,128)(2,1)} fusion(bf16[3456,2048]{1,0:T(8,128)(2,1)} %get-tuple-element.48, bf16[3456,512]{1,0:T(8,128)(2,1)} %bitcast.27), kind=kOutput, calls=%fused_computation.36 | convolution fusion | flops 7248805888 | bytes 19791872 | tf_op jit(solution)/shard_map/rh,rd->hd/dot_general | solution.py:182
  397.7 13.0 %fusion.8 = bf16[1,512,2048]{2,1,0:T(8,128)(2,1)} fusion(bf16[3456,512]{1,0:T(8,128)(2,1)} %bitcast.19, bf16[3456,2048]{1,0:T(8,128)(2,1)} %get-tuple-element.68), kind=kOutput, calls=%fused_computation.37 | convolution fusion | flops 7248805888 | bytes 19791872 | tf_op jit(solution)/shard_map/rd,rh->dh/dot_general | solution.py:186
  410.7 9.1 %gather_fusion = bf16[1970,512]{1,0:T(8,128)(2,1)} fusion(bf16[3456,512]{1,0:T(8,128)(2,1)S(1)} %bitcast.112, s32[2048]{0:T(1024)S(1)} %pad_clamp_fusion), kind=kCustom, calls=%fused_computation | custom fusion | bytes 4042440 | tf_op jit(solution)/shard_map/gather | solution.py:152
  419.9 5.6 reshape.306
  425.5 13.6 %multiply_reduce_fusion.3 = (f32[985,2]{1,0:T(8,128)S(1)}, f32[985,512]{1,0:T(8,128)}) fusion(f32[985,2,512]{2,1,0:T(2,128)} %reshape.306, f32[985,512]{1,0:T(8,128)S(1)} %copy-done.7, f32[985,2]{1,0:T(8,128)S(1)} %copy-done.23), kind=kLoop, calls=%fused_computation.31 | loop fusion | flops 3528270 | bytes 8084880 | tf_op jit(solution)/shard_map/reduce_sum | solution.py:162
  439.4 23.3 %all-to-all-done.3 = bf16[8,432,512]{2,1,0:T(8,128)(2,1)} async-done(((bf16[8,432,512]{2,1,0:T(8,128)(2,1)}), bf16[8,432,512]{2,1,0:T(8,128)(2,1)}, u32[]{:S(2)}, u32[]{:S(2)}) %all-to-all-start.3) | async-done | bytes 3538976 | tf_op jit(solution)/shard_map/all_to_all | solution.py:193
  462.7 10.4 %gather_fusion.1 = bf16[1970,512]{1,0:T(8,128)(2,1)S(1)} fusion(bf16[3456,512]{1,0:T(8,128)(2,1)} %bitcast.29, s32[2048]{0:T(1024)S(1)} %pad_clamp_fusion), kind=kCustom, calls=%fused_computation.1 | custom fusion | bytes 4042440 | tf_op jit(solution)/shard_map/gather | solution.py:195
  473.1 4.7 reshape.309
  477.8 8.4 %reduce_sum.274 = f32[985,512]{1,0:T(8,128)} reduce(f32[985,2,512]{2,1,0:T(2,128)} %reshape.309, f32[]{:T(128)} %constant.40.clone.1), dimensions={1}, to_apply=%region_15.16 | reduce | flops 504320 | bytes 6051844 | tf_op jit(solution)/shard_map/reduce_sum | solution.py:201
  486.3 4.2 multiply_reduce_fusion.6
  495.9 4.2 copy.119
  500.2 3.4 convolution_convert_fusion.7
  503.6 6.7 multiply_reduce_fusion.1
  510.3 4.7 multiply_convert_fusion.1
  517.6 2.9 fusion.49
  520.6 4.3 fusion.48
  524.8 4.1 copy.129
  528.9 4.0 reshape.300
  532.9 4.0 copy.126
  536.9 4.0 reshape.299
  540.8 2.7 copy.123
  543.5 4.0 reshape.298
  552.0 3.3 convolution_convert_fusion.2
  563.9 38.0 %pmax.7 = f32[8]{0:T(128)S(1)} all-reduce(f32[8]{0:T(128)S(1)} %get-tuple-element.17), channel_id=1, replica_groups=mesh['expert'=8,'fsdp'=4] {'expert','fsdp'}, use_global_device_ids=true, to_apply=%region_58.59 | all-reduce | flops 8 | bytes 64 | tf_op jit(solution)/shard_map/pmax | solution.py:318
  604.4 6.5 multiply_reduce_fusion.7
  611.0 3.7 multiply_add_fusion
  615.1 6.4 all-reduce.10
  622.0 3.2 reshape.301
  627.2 4.5 reduce-scatter.22.cloned.1.call-done
  632.5 21.7 %all-reduce.8 = (bf16[128]{0:T(256)(128)(2,1)S(1)}, bf16[128]{0:T(256)(128)(2,1)S(1)}, bf16[128]{0:T(256)(128)(2,1)S(1)}, bf16[128]{0:T(256)(128)(2,1)S(1)}, bf1...) all-reduce(bf16[128]{0:T(256)(128)(2,1)S(1)} %dynamic-slice.1, ...), channel_id=1, replica_groups=mesh['expert'=8,'fsdp'=4] {'expert'}, use_global_device_ids=true, to_apply=%region_26.27 | all-reduce | flops 1920 | bytes 7680 | tf_op jit(solution)/shard_map/psum | solution.py:293
  658.4 49.8 %all-reduce.13.cloned.1.call-done = (bf16[128,1536]{1,0:T(8,128)(2,1)}, bf16[128,512]{1,0:T(8,128)(2,1)}) async-done(((bf16[128,1536]{1,0:T(8,128)(2,1)}, bf16[128,512]{1,0:T(8,128)(2,1)}), (bf16[128,1536]{1,0:T(8,128)(2,1)}, bf16[128,512]{1,0:T(8,128)(2,1)})) %all-reduce.13.cloned.1.call-update) | async-done | bytes 524304 | tf_op jit(solution)/shard_map/psum | solution.py:295
  (294 shorter events, 73.5 us)
Async XLA Ops:
  7.2 10.6 %copy-start.67 = (bf16[128]{0:T(256)(128)(2,1)S(1)}, bf16[128]{0:T(256)(128)(2,1)}, u32[]{:S(2)}) copy-start(bf16[128]{0:T(256)(128)(2,1)} %param.20) | copy-start | bytes 772
  7.2 15.9 %copy-start.68 = (bf16[128]{0:T(256)(128)(2,1)S(1)}, bf16[128]{0:T(256)(128)(2,1)}, u32[]{:S(2)}) copy-start(bf16[128]{0:T(256)(128)(2,1)} %param.23) | copy-start | bytes 772
  7.2 20.9 %copy-start.69 = (bf16[128]{0:T(256)(128)(2,1)S(1)}, bf16[128]{0:T(256)(128)(2,1)}, u32[]{:S(2)}) copy-start(bf16[128]{0:T(256)(128)(2,1)} %param.22) | copy-start | bytes 772
  7.2 25.9 %copy-start.70 = (bf16[128]{0:T(256)(128)(2,1)S(1)}, bf16[128]{0:T(256)(128)(2,1)}, u32[]{:S(2)}) copy-start(bf16[128]{0:T(256)(128)(2,1)} %param.25) | copy-start | bytes 772
  7.3 31.0 %copy-start.71 = (bf16[128]{0:T(256)(128)(2,1)S(1)}, bf16[128]{0:T(256)(128)(2,1)}, u32[]{:S(2)}) copy-start(bf16[128]{0:T(256)(128)(2,1)} %param.26) | copy-start | bytes 772
  7.3 36.0 %copy-start.72 = (bf16[128]{0:T(256)(128)(2,1)S(1)}, bf16[128]{0:T(256)(128)(2,1)}, u32[]{:S(2)}) copy-start(bf16[128]{0:T(256)(128)(2,1)} %param.27) | copy-start | bytes 772
  7.3 41.0 %copy-start.44 = (s32[985,2]{0,1:T(2,128)S(1)}, s32[985,2]{0,1:T(2,128)}, u32[]{:S(2)}) copy-start(s32[985,2]{0,1:T(2,128)} %param.33) | copy-start | bytes 23644
  7.3 53.0 %all-gather.11.cloned.1.call-start = ((), (), s32[]{:S(2)}) async-start(), calls=%async_computation.11 | async-start | bytes 1966080 | tf_op jit(solution)/shard_map/all_gather | solution.py:55
  9.5 42.8 %copy-start.46 = (bf16[128,512]{1,0:T(8,128)(2,1)S(1)}, bf16[128,512]{1,0:T(8,128)(2,1)}, u32[]{:S(2)}) copy-start(bf16[128,512]{1,0:T(8,128)(2,1)} %param.24) | copy-start | bytes 393220
  11.0 52.5 %copy-start.4 = (f32[985,512]{1,0:T(8,128)}, f32[985,512]{1,0:T(8,128)S(1)}, u32[]{:S(2)}) copy-start(f32[985,512]{1,0:T(8,128)S(1)} %reshape.278) | copy-start | bytes 6051844
  11.1 52.4 %copy-start.40 = (f32[985]{0:T(1024)}, f32[985]{0:T(1024)S(1)}, u32[]{:S(2)}) copy-start(f32[985]{0:T(1024)S(1)} %div.38) | copy-start | bytes 11824
  11.8 51.7 %copy-start.42 = (f32[985]{0:T(1024)}, f32[985]{0:T(1024)S(1)}, u32[]{:S(2)}) copy-start(f32[985]{0:T(1024)S(1)} %rsqrt.20) | copy-start | bytes 11824
  17.8 45.7 %copy-start.47 = (f32[4,1,128]{2,1,0:T(1,128)}, f32[4,1,128]{2,1,0:T(1,128)S(1)}, u32[]{:S(2)}) copy-start(f32[4,1,128]{2,1,0:T(1,128)S(1)} %convert_element_type.334) | copy-start | bytes 6148
  23.1 40.4 %copy-start.55 = (f32[4,1,128]{2,1,0:T(1,128)}, f32[4,1,128]{2,1,0:T(1,128)S(1)}, u32[]{:S(2)}) copy-start(f32[4,1,128]{2,1,0:T(1,128)S(1)} %convert_element_type.335) | copy-start | bytes 6148
  43.3 114.8 %copy-start.51 = (f32[4,1,128]{2,1,0:T(1,128)}, f32[4,1,128]{2,1,0:T(1,128)S(1)}, u32[]{:S(2)}) copy-start(f32[4,1,128]{2,1,0:T(1,128)S(1)} %convert_element_type.339) | copy-start | bytes 6148
  48.3 109.7 %copy-start.61 = (f32[4,1,128]{2,1,0:T(1,128)}, f32[4,1,128]{2,1,0:T(1,128)S(1)}, u32[]{:S(2)}) copy-start(f32[4,1,128]{2,1,0:T(1,128)S(1)} %convert_element_type.340) | copy-start | bytes 6148
  60.2 101.0 %copy-start.59 = (s32[1970,1]{0,1:T(1,128)}, s32[1970,1]{0,1:T(1,128)S(1)}, u32[]{:S(2)}) copy-start(s32[1970,1]{0,1:T(1,128)S(1)} %compare_select_fusion) | copy-start | bytes 23644
  99.6 58.5 %copy-start.1 = (f32[985,512]{1,0:T(8,128)}, f32[985,512]{1,0:T(8,128)S(1)}, u32[]{:S(2)}) copy-start(f32[985,512]{1,0:T(8,128)S(1)} %get-tuple-element.56) | copy-start | bytes 6051844
  99.6 58.5 %copy-start.36 = (f32[985]{0:T(1024)}, f32[985]{0:T(1024)S(1)}, u32[]{:S(2)}) copy-start(f32[985]{0:T(1024)S(1)} %broadcast_multiply_fusion.6) | copy-start | bytes 11824
  100.0 58.0 %copy-start.38 = (f32[985]{0:T(1024)}, f32[985]{0:T(1024)S(1)}, u32[]{:S(2)}) copy-start(f32[985]{0:T(1024)S(1)} %add_rsqrt_fusion.1) | copy-start | bytes 11824
  121.6 7.5 %copy-start.31 = (bf16[5,197,512]{2,1,0:T(8,128)(2,1)S(1)}, bf16[5,197,512]{2,1,0:T(8,128)(2,1)}, u32[]{:S(2)}) copy-start(bf16[5,197,512]{2,1,0:T(8,128)(2,1)} %param.35) | copy-start | bytes 3025924
  121.6 85.7 %all-to-all-start = ((bf16[8,432,512]{2,1,0:T(8,128)(2,1)}), bf16[8,432,512]{2,1,0:T(8,128)(2,1)}, u32[]{:S(2)}, u32[]{:S(2)}) async-start(bf16[8,432,512]{2,1,0:T(8,128)(2,1)} %bitcast.113), calls=%async_computation | async-start | bytes 7077888 | tf_op jit(solution)/shard_map/all_to_all | solution.py:141
  127.6 84.4 %all-gather.13.cloned.1.call-start = ((), (), s32[]{:S(2)}) async-start(), calls=%async_computation.12 | async-start | bytes 2621440 | tf_op jit(solution)/shard_map/all_gather | solution.py:63
  128.3 154.5 %all-gather.15.cloned.1.call-start = ((), (), s32[]{:S(2)}) async-start(), calls=%async_computation.13 | async-start | bytes 2621440 | tf_op jit(solution)/shard_map/all_gather | solution.py:65
  135.4 6.1 copy-start.63
  135.4 11.3 %copy-start.73 = (bf16[1,128]{1,0:T(2,128)(2,1)S(1)}, bf16[1,128]{1,0:T(2,128)(2,1)}, u32[]{:S(2)}) copy-start(bf16[1,128]{1,0:T(2,128)(2,1)} %param.32) | copy-start | bytes 772
  135.5 17.0 %copy-start.64 = (bf16[128,8]{0,1:T(8,128)(2,1)S(1)}, bf16[128,8]{0,1:T(8,128)(2,1)}, u32[]{:S(2)}) copy-start(bf16[128,8]{0,1:T(8,128)(2,1)} %param.28) | copy-start | bytes 6148
  158.0 21.7 %copy-start.49 = (bf16[512,8]{0,1:T(8,128)(2,1)}, bf16[512,8]{0,1:T(8,128)(2,1)S(1)}, u32[]{:S(2)}) copy-start(bf16[512,8]{0,1:T(8,128)(2,1)S(1)} %all_gather.51) | copy-start | bytes 24580
  159.5 20.3 %copy-start.53 = (f32[985]{0:T(1024)}, f32[985]{0:T(1024)S(1)}, u32[]{:S(2)}) copy-start(f32[985]{0:T(1024)S(1)} %get-tuple-element.58) | copy-start | bytes 11824
  159.5 20.2 %copy-start.57 = (f32[985]{0:T(1024)}, f32[985]{0:T(1024)S(1)}, u32[]{:S(2)}) copy-start(f32[985]{0:T(1024)S(1)} %fusion.38) | copy-start | bytes 11824
  160.9 18.8 %copy-start.22 = (f32[985,2]{1,0:T(8,128)}, f32[985,2]{1,0:T(8,128)S(1)}, u32[]{:S(2)}) copy-start(f32[985,2]{1,0:T(8,128)S(1)} %copy.114) | copy-start | bytes 23644
  207.3 88.1 %all-to-all-start.2 = ((bf16[8,432,512]{2,1,0:T(8,128)(2,1)}), bf16[8,432,512]{2,1,0:T(8,128)(2,1)}, u32[]{:S(2)}, u32[]{:S(2)}) async-start(bf16[8,432,512]{2,1,0:T(8,128)(2,1)} %bitcast.26), calls=%async_computation.2 | async-start | bytes 7077888 | tf_op jit(solution)/shard_map/all_to_all | solution.py:174
  212.0 70.8 %copy-start.65 = (f32[1,512]{1,0:T(1,128)S(1)}, f32[1,512]{1,0:T(1,128)}, u32[]{:S(2)}) copy-start(f32[1,512]{1,0:T(1,128)} %add.210) | copy-start | bytes 6148
  295.4 84.2 %all-to-all-start.1 = ((bf16[8,432,512]{2,1,0:T(8,128)(2,1)}), bf16[8,432,512]{2,1,0:T(8,128)(2,1)S(1)}, u32[]{:S(2)}, u32[]{:S(2)}) async-start(bf16[8,432,512]{2,1,0:T(8,128)(2,1)} %bitcast.115), calls=%async_computation.1 | async-start | bytes 7077888 | tf_op jit(solution)/shard_map/all_to_all | solution.py:150
  301.4 255.3 %reduce-scatter.26.cloned.1.call-start = ((), (), s32[]{:S(2)}) async-start(), calls=%async_computation.20 | async-start | bytes 163840
  304.8 253.3 %reduce-scatter.24.cloned.1.call-start = ((), (), s32[]{:S(2)}) async-start(), calls=%async_computation.19 | async-start | bytes 655360
  379.6 83.1 %all-to-all-start.3 = ((bf16[8,432,512]{2,1,0:T(8,128)(2,1)}), bf16[8,432,512]{2,1,0:T(8,128)(2,1)}, u32[]{:S(2)}, u32[]{:S(2)}) async-start(bf16[8,432,512]{2,1,0:T(8,128)(2,1)} %bitcast.114), calls=%async_computation.3 | async-start | bytes 7077888 | tf_op jit(solution)/shard_map/all_to_all | solution.py:193
  384.1 13.6 %copy-start.60 = (s32[1970,1]{0,1:T(1,128)S(1)}, s32[1970,1]{0,1:T(1,128)}, u32[]{:S(2)}) copy-start(s32[1970,1]{0,1:T(1,128)} %copy-done.59) | copy-start | bytes 23644
  384.1 175.5 %reduce-scatter.20.cloned.1.call-start = ((), (), s32[]{:S(2)}) async-start(), calls=%async_computation.17 | async-start | bytes 2621440 | tf_op jit(solution)/shard_map/reduce_scatter | solution.py:311
  397.2 164.6 %reduce-scatter.18.cloned.1.call-start = ((), (), s32[]{:S(2)}) async-start(), calls=%async_computation.16 | async-start | bytes 2621440 | tf_op jit(solution)/shard_map/reduce_scatter | solution.py:305
  410.7 204.2 %reduce-scatter.16.cloned.1.call-start = ((), (), s32[]{:S(2)}) async-start(), calls=%async_computation.15 | async-start | bytes 655360 | tf_op jit(solution)/shard_map/reduce_scatter | solution.py:276
  419.9 5.6 copy-start.23
  425.5 13.8 %copy-start.45 = (s32[985,2]{0,1:T(2,128)S(1)}, s32[985,2]{0,1:T(2,128)}, u32[]{:S(2)}) copy-start(s32[985,2]{0,1:T(2,128)} %param.33) | copy-start | bytes 23644
  425.5 13.8 %copy-start.35 = (f32[985,8]{0,1:T(8,128)S(1)}, f32[985,8]{0,1:T(8,128)}, u32[]{:S(2)}) copy-start(f32[985,8]{0,1:T(8,128)} %copy-done.34) | copy-start | bytes 94564
  425.5 13.8 %copy-start.54 = (f32[985]{0:T(1024)S(1)}, f32[985]{0:T(1024)}, u32[]{:S(2)}) copy-start(f32[985]{0:T(1024)} %copy-done.53) | copy-start | bytes 11824
  425.5 13.8 %copy-start.58 = (f32[985]{0:T(1024)S(1)}, f32[985]{0:T(1024)}, u32[]{:S(2)}) copy-start(f32[985]{0:T(1024)} %copy-done.57) | copy-start | bytes 11824
  477.8 8.4 %copy-start.2 = (f32[985,512]{1,0:T(8,128)S(1)}, f32[985,512]{1,0:T(8,128)}, u32[]{:S(2)}) copy-start(f32[985,512]{1,0:T(8,128)} %copy-done.1) | copy-start | bytes 6051844
  477.8 8.4 %copy-start.33 = (f32[985,8]{0,1:T(8,128)S(1)}, f32[985,8]{0,1:T(8,128)}, u32[]{:S(2)}) copy-start(f32[985,8]{0,1:T(8,128)} %copy-done.32) | copy-start | bytes 94564
  477.8 8.4 %copy-start.37 = (f32[985]{0:T(1024)S(1)}, f32[985]{0:T(1024)}, u32[]{:S(2)}) copy-start(f32[985]{0:T(1024)} %copy-done.36) | copy-start | bytes 11824
  477.8 8.4 %copy-start.39 = (f32[985]{0:T(1024)S(1)}, f32[985]{0:T(1024)}, u32[]{:S(2)}) copy-start(f32[985]{0:T(1024)} %copy-done.38) | copy-start | bytes 11824
  477.8 8.4 %copy-start.50 = (bf16[512,8]{0,1:T(8,128)(2,1)S(1)}, bf16[512,8]{0,1:T(8,128)(2,1)}, u32[]{:S(2)}) copy-start(bf16[512,8]{0,1:T(8,128)(2,1)} %copy-done.49) | copy-start | bytes 24580
  477.8 8.4 %copy-start.52 = (f32[4,1,128]{2,1,0:T(1,128)S(1)}, f32[4,1,128]{2,1,0:T(1,128)}, u32[]{:S(2)}) copy-start(f32[4,1,128]{2,1,0:T(1,128)} %copy-done.51) | copy-start | bytes 6148
  495.9 7.7 %copy-start.13 = (bf16[5,197,8,64]{1,3,2,0:T(8,128)(2,1)S(1)}, bf16[5,197,8,64]{1,3,2,0:T(8,128)(2,1)}, u32[]{:S(2)}) copy-start(bf16[5,197,8,64]{1,3,2,0:T(8,128)(2,1)} %copy-done.12) | copy-start | bytes 3025924
  495.9 7.7 %copy-start.30 = (f32[5,8,197]{2,1,0:T(8,128)S(1)}, f32[5,8,197]{2,1,0:T(8,128)}, u32[]{:S(2)}) copy-start(f32[5,8,197]{2,1,0:T(8,128)} %copy-done.29) | copy-start | bytes 94564
  503.6 14.0 %slice-start = ((s8[8192000]{0:T(1024)(128)(4,1)}), s8[4194304]{0:T(1024)(128)(4,1)S(1)}, s32[]{:S(2)}) async-start(s8[8192000]{0:T(1024)(128)(4,1)} %bitcast.110), calls=%async_computation.22 | async-start | bytes 8388608
  510.3 7.3 %slice-start.1 = ((s8[8192000]{0:T(1024)(128)(4,1)}), s8[3997696]{0:T(1024)(128)(4,1)S(1)}, s32[]{:S(2)}) async-start(s8[8192000]{0:T(1024)(128)(4,1)} %bitcast.110), calls=%async_computation.23 | async-start | bytes 7995392
  520.5 94.3 %reduce-scatter.14.cloned.1.call-start = ((), (), s32[]{:S(2)}) async-start(), calls=%async_computation.14 | async-start | bytes 1966080 | tf_op jit(solution)/shard_map/reduce_scatter | solution.py:267
  532.9 7.9 %copy-start.19 = (bf16[5,197,8,64]{1,3,2,0:T(8,128)(2,1)S(1)}, bf16[5,197,8,64]{1,3,2,0:T(8,128)(2,1)}, u32[]{:S(2)}) copy-start(bf16[5,197,8,64]{1,3,2,0:T(8,128)(2,1)} %get-tuple-element.64) | copy-start | bytes 3025924
  543.5 6.8 copy-start.26
  555.3 46.7 %copy-start.62 = (f32[4,1,128]{2,1,0:T(1,128)S(1)}, f32[4,1,128]{2,1,0:T(1,128)}, u32[]{:S(2)}) copy-start(f32[4,1,128]{2,1,0:T(1,128)} %copy-done.61) | copy-start | bytes 6148
  555.3 76.4 %reduce-scatter.22.cloned.1.call-start = ((), (), s32[]{:S(2)}) async-start(), calls=%async_computation.18 | async-start | bytes 163840
  604.4 6.6 copy-start.6
  610.9 97.3 %all-reduce.13.cloned.1.call-start = ((), (), s32[]{:S(2)}) async-start(), calls=%async_computation.21 | async-start | bytes 1048576 | tf_op jit(solution)/shard_map/psum | solution.py:295
  614.7 10.5 %copy-start.24 = (bf16[985,512]{1,0:T(8,128)(2,1)S(1)}, bf16[985,512]{1,0:T(8,128)(2,1)}, u32[]{:S(2)}) copy-start(bf16[985,512]{1,0:T(8,128)(2,1)} %get-tuple-element.52) | copy-start | bytes 3025924
  (29 other events, 100.3 us)
Sparse Core Ops, SparseCore 0:
  9.7 22.3 all-gather.10
  130.0 24.0 all-gather.12
  155.6 22.5 all-gather.14
  304.9 21.0 reduce-scatter.25
  338.2 23.0 reduce-scatter.23
  397.3 32.7 reduce-scatter.19
  432.8 31.4 reduce-scatter.17
  520.6 20.7 reduce-scatter.15
  555.4 27.4 reduce-scatter.13
  611.0 20.5 reduce-scatter.21
  635.5 72.6 all-reduce.12
where the time goes:
time: 726 us; the launch traced here: 719 us
  matrix products  204 us (28%)
  local copies, waits for them, and re-layouts  138 us (19%)
  waiting for transfers between devices  136 us (19%)
  blocking collectives  126 us (17%)
  other arithmetic  76 us (10%)
  starting transfers between devices  22.2 us (3%)
  between operations  16.1 us (2%)
    dot_general x1, matrix products, shards(): jnp.dot(flat_in, first_weight, preferred_element_type=jnp.float32)  70.8 us
    psum x1, waiting for transfers between devices, shards(): lax.psum(shares[2].astype(jnp.bfloat16), 'expert').astype(jnp.float32)  49.8 us
    pmax x1, blocking collectives, shards(): peak_logit = lax.pmax(head_peak, ('expert', 'fsdp'))  38 us
    dot_general x1, matrix products, shards(): jnp.einsum('rd,hd->rh', flat_grad, second_weight, preferred_element_type=...  31.9 us
    all_to_all x1, waiting for transfers between devices, shards(): lax.all_to_all(produced, 'expert', split_axis=0, concat_axis=0, tiled=True)  28.8 us
    all_to_all x1, waiting for transfers between devices, shards(): lax.all_to_all(outgoing, 'expert', split_axis=0, concat_axis=0, tiled=True)  27.6 us
    all_to_all x1, waiting for transfers between devices, shards(): lax.all_to_all(row_grad, 'expert', split_axis=0, concat_axis=0, tiled=True)  23.3 us
    psum x1, blocking collectives, shards(): lax.psum(shares[0].astype(jnp.bfloat16), 'expert').astype(jnp.float32)  21.7 us
  transfers between devices with their start and end apart: 15, of which 5 were waited for; matrix products, arithmetic and copies ran while one was open for 49% of the time, Pallas kernels for 0%

commit v1 on v0

--- a/solution.py
+++ b/solution.py
@@ -1,3 +1,4 @@
+import functools
 import jax
 import jax.numpy as jnp
 from jax import lax
@@ -6,6 +7,26 @@
 HEADS = 8
 norm_eps = 1e-06
 highest = lax.Precision.HIGHEST
+
+
+def apply_sums_all_on_mesh(mine_x, axis_tag):
+    tmp, aux = (lax.axis_size(axis_tag), lax.axis_index(axis_tag))
+    z1 = mine_x.shape[0] // tmp
+    x_now = jnp.roll(mine_x, -aux * z1, axis=0)
+    rack = [lax.slice_in_dim(x_now, 0, z1, axis=0)]
+    for tick in range(1, tmp):
+        plain = lax.slice_in_dim(x_now, tick * z1, (tick + 1) * z1, axis=0)
+        rack.append(
+            lax.ppermute(
+                plain, axis_name=axis_tag, perm=[(w, (w + tick) % tmp) for w in range(tmp)]
+            )
+        )
+    block_last = jnp.concatenate(rack[::-1], axis=0)
+    clean = jnp.roll(block_last, (aux + 1) * rack[0].shape[0], axis=0)
+    return clean
+
+
+treat_bands = functools.partial(apply_sums_all_on_mesh, axis_tag="expert")
 
 
 def layer_norm(matrix, norm_gain, norm_shift):
@@ -138,7 +159,7 @@
         .set(slot_rows)
         .reshape(expert_total, capacity, feature_width)
     )
-    arrived = lax.all_to_all(outgoing, "expert", split_axis=0, concat_axis=0, tiled=True)
+    arrived = treat_bands(outgoing)
     flat_in = arrived.reshape(-1, feature_width)
     activation = gelu_exact(
         jnp.dot(flat_in, first_weight, preferred_element_type=jnp.float32) + first_bias

time: 726 us -> 807 us (1.11)
  waiting for transfers between devices: 136 us -> 182 us
  starting transfers between devices: 22.2 us -> 42.9 us
  local copies, waits for them, and re-layouts: 138 us -> 154 us
    ppermute x0 -> x7, waiting for transfers between devices: none -> 97.6 us  [apply_sums_all_on_mesh(): lax.ppermute(plain, axis_name=axis_tag, perm=[(w, (w + tick) % tmp) for w...]
    ppermute x0 -> x7, starting transfers between devices: none -> 29 us  [apply_sums_all_on_mesh(): lax.ppermute(plain, axis_name=axis_tag, perm=[(w, (w + tick) % tmp) for w...]
    all_to_all x1 -> x0, waiting for transfers between devices: 27.6 us -> none  [shards(): lax.all_to_all(outgoing, 'expert', split_axis=0, concat_axis=0, tiled=True)]
    psum x1, waiting for transfers between devices: 49.8 us -> 38.5 us  [shards(): lax.psum(shares[2].astype(jnp.bfloat16), 'expert').astype(jnp.float32)]
    unnamed x175 -> x182, local copies, waits for them, and re-layouts: 15.2 us -> 25.1 us
    all_to_all x1, waiting for transfers between devices: 23.3 us -> 13.6 us  [shards(): lax.all_to_all(row_grad, 'expert', split_axis=0, concat_axis=0, tiled=True)]
  transfers between devices with their start and end apart: 15 -> 21, of which waited for: 5 -> 5; matrix products, arithmetic and copies ran while one was open for 49% -> 52% of each run, Pallas kernels for 0% -> 0%
where the time goes in v1:
time: 807 us; the launch traced here: 801 us
  matrix products  198 us (25%)
  waiting for transfers between devices  182 us (23%)
  local copies, waits for them, and re-layouts  154 us (19%)
  blocking collectives  126 us (16%)
  other arithmetic  82.9 us (10%)
  starting transfers between devices  42.9 us (5%)
  between operations  15.9 us (2%)
    ppermute x7, waiting for transfers between devices, apply_sums_all_on_mesh(): lax.ppermute(plain, axis_name=axis_tag, perm=[(w, (w + tick) % tmp) for w...  97.6 us
    dot_general x1, matrix products, shards(): jnp.dot(flat_in, first_weight, preferred_element_type=jnp.float32)  68 us
    psum x1, waiting for transfers between devices, shards(): lax.psum(shares[2].astype(jnp.bfloat16), 'expert').astype(jnp.float32)  38.5 us
    pmax x1, blocking collectives, shards(): peak_logit = lax.pmax(head_peak, ('expert', 'fsdp'))  37.2 us
    dot_general x1, matrix products, shards(): jnp.einsum('rd,hd->rh', flat_grad, second_weight, preferred_element_type=...  32 us
    all_to_all x1, waiting for transfers between devices, shards(): lax.all_to_all(produced, 'expert', split_axis=0, concat_axis=0, tiled=True)  29.6 us
    ppermute x7, starting transfers between devices, apply_sums_all_on_mesh(): lax.ppermute(plain, axis_name=axis_tag, perm=[(w, (w + tick) % tmp) for w...  29 us
    unnamed x182, local copies, waits for them, and re-layouts  25.1 us
  transfers between devices with their start and end apart: 21, of which 5 were waited for; matrix products, arithmetic and copies ran while one was open for 52% of the time, Pallas kernels for 0%

profile of v1, /device:TPU:0, one launch (start us, length us, event | category | flops | bytes accessed | tf_op | source)
XLA Modules:
  0.0 801.0 jit_solution(8937736740194227322)
XLA Ops:
  14.2 6.0 all-gather
  20.2 5.3 all-gather.1
  25.5 5.0 all-gather.3
  30.6 5.0 all-gather.2
  35.6 5.0 all-gather.4
  40.6 5.0 all-gather.5
  45.7 5.0 all-gather.6
  50.7 5.0 all_gather.55
  56.3 5.1 all_gather.51
  61.5 5.1 all_gather.53
  72.8 10.3 %all_gather.47 = bf16[512,512]{1,0:T(8,128)(2,1)} all-gather(bf16[128,512]{1,0:T(8,128)(2,1)S(1)} %copy-done.45), channel_id=1, replica_groups=mesh['expert'=8,'fsdp'=4] {'fsdp'}, dimensions={0}, use_global_device_ids=true | all-gather | bytes 655360 | tf_op jit(solution)/shard_map/all_gather | solution.py:79
  83.1 2.8 reshape.308
  85.9 4.9 mul.251
  90.7 5.9 mul.252
  96.7 3.2 fusion.46
  104.9 4.0 copy.109
  111.3 3.1 copy.110
  114.4 4.1 reshape.279
  118.5 4.4 copy.111
  131.1 2.7 copy.113
  133.8 3.1 reshape.282
  145.5 13.4 %scatter_custom_fusion = bf16[3456,512]{1,0:T(8,128)(2,1)} fusion(s32[1970]{0:T(1024)S(1)} %bitcast.138, bf16[1970,512]{1,0:T(8,128)(2,1)} %reshape.330, bf16[]{:T(256)} %constant.33.clone.1), kind=kCustom, calls=%fused_computation.75 | custom fusion | bytes 3539456 | tf_op jit(solution)/shard_map/scatter | solution.py:159
  158.8 3.3 fusion.8
  163.8 3.4 collective-permute-start.2
  174.5 18.4 %scatter_custom_fusion.1 = bf16[3456,512]{1,0:T(8,128)(2,1)} fusion(s32[1970]{0:T(1024)} %bitcast.139, f32[1970,512]{1,0:T(8,128)} %mul.252, f32[1970]{0:T(1024)S(1)} %mul.249, bf16[]{:T(256)} %constant.33.clone.1), kind=kCustom, calls=%fused_computation.69 | custom fusion | flops 2017280 | bytes 7594184 | tf_op jit(solution)/shard_map/scatter | solution.py:192
  193.0 4.5 all-to-all-start.1
  199.4 19.1 %collective-permute-start.4 = (bf16[1,432,512]{2,1,0:T(8,128)(2,1)}, bf16[1,432,512]{2,1,0:T(8,128)(2,1)S(1)}, u32[]{:S(2)}, u32[]{:S(2)}) collective-permute-start(bf16[1,432,512]{2,1,0:T(8,128)(2,1)} %get-tuple-element.55), channel_id=1, source_target_pairs={{0,12},{4,16},{8,20},{12,24},{16,28},{20,0},{24,4},{28,8},{1,13},{... | collective-permute-start | bytes 1327112 | tf_op jit(solution)/shard_map/ppermute | solution.py:20
  221.9 14.0 %collective-permute-done.3 = bf16[1,432,512]{2,1,0:T(8,128)(2,1)} collective-permute-done((bf16[1,432,512]{2,1,0:T(8,128)(2,1)}, bf16[1,432,512]{2,1,0:T(8,128)(2,1)}, u32[]{:S(2)}, u32[]{:S(2)}) %collective-permute-start.3) | collective-permute-done | bytes 442400 | tf_op jit(solution)/shard_map/ppermute | solution.py:20
  237.0 83.6 %collective-permute-done.4 = bf16[1,432,512]{2,1,0:T(8,128)(2,1)S(1)} collective-permute-done((bf16[1,432,512]{2,1,0:T(8,128)(2,1)}, bf16[1,432,512]{2,1,0:T(8,128)(2,1)S(1)}, u32[]{:S(2)}, u32[]{:S(2)}) %collective-permute-start.4) | collective-permute-done | bytes 442400 | tf_op jit(solution)/shard_map/ppermute | solution.py:20
  322.1 68.0 %multiply_convert_fusion = (bf16[3456,2048]{1,0:T(8,128)(2,1)}, f32[3456,2048]{1,0:T(8,128)}, f32[3456,2048]{1,0:T(8,128)}) fusion(f32[2048]{0:T(1024)S(1)} %bitcast.148, bf16[3456,512]{1,0:T(8,128)(2,1)S(1)} %bitcast.118, bf16[1,512,2048]{2,1,0:T(8,128)(2,1)} %all-gather.13.cloned.1.call-done), kind=kOutput, calls=%fused_computation.7 | convolution fusion | flops 7714897920 | bytes 76423168 | tf_op jit(solution)/shard_map/dot_general | solution.py:165
  390.1 12.5 %add_convert_fusion.1 = bf16[3456,512]{1,0:T(8,128)(2,1)} fusion(bf16[3456,2048]{1,0:T(8,128)(2,1)} %get-tuple-element.49, f32[512]{0:T(512)S(1)} %bitcast.150, bf16[1,2048,512]{2,1,0:T(8,128)(2,1)} %all-gather.15.cloned.1.call-done), kind=kOutput, calls=%fused_computation.29 | convolution fusion | flops 7251296256 | bytes 19793920 | tf_op jit(solution)/shard_map/dot_general | solution.py:168
  402.6 4.5 all-to-all-start
  411.0 32.0 %fusion.53 = (bf16[2048]{0:T(1024)(128)(2,1)S(1)}, bf16[3456,2048]{1,0:T(8,128)(2,1)}) fusion(f32[3456,2048]{1,0:T(8,128)} %get-tuple-element.50, bf16[3456,512]{1,0:T(8,128)(2,1)} %bitcast.27, bf16[1,2048,512]{2,1,0:T(8,128)(2,1)} %all-gather.15.cloned.1.call-done, f32[3456,2048]{1,0:T(8,128)} %get-tuple-element.65, f32[2048]{0:T(1024)S(1)} %bitcast.149), kind=kOutput, calls=%fused_computation.153 | convolution fusion | flops 7361001472 | bytes 76427264 | tf_op jit(solution)/shard_map/rd,hd->rh/dot_general | solution.py:205
  444.2 12.7 %convolution_convert_fusion = bf16[3456,512]{1,0:T(8,128)(2,1)} fusion(bf16[3456,2048]{1,0:T(8,128)(2,1)} %get-tuple-element.76, bf16[1,512,2048]{2,1,0:T(8,128)(2,1)} %all-gather.13.cloned.1.call-done), kind=kOutput, calls=%fused_computation.32 | convolution fusion | flops 7249526784 | bytes 19791872 | tf_op jit(solution)/shard_map/rh,dh->rd/dot_general | solution.py:210
  456.8 29.6 %all-to-all-done = bf16[8,432,512]{2,1,0:T(8,128)(2,1)S(1)} async-done(((bf16[8,432,512]{2,1,0:T(8,128)(2,1)}), bf16[8,432,512]{2,1,0:T(8,128)(2,1)S(1)}, u32[]{:S(2)}, u32[]{:S(2)}) %all-to-all-start) | async-done | bytes 3538976 | tf_op jit(solution)/shard_map/all_to_all | solution.py:171
  488.2 3.7 all-to-all-start.2
  492.1 11.6 %gather_fusion = bf16[1970,512]{1,0:T(8,128)(2,1)} fusion(bf16[3456,512]{1,0:T(8,128)(2,1)} %bitcast.115, s32[2048]{0:T(1024)S(1)} %copy-done.50), kind=kCustom, calls=%fused_computation | custom fusion | bytes 4042440 | tf_op jit(solution)/shard_map/gather | solution.py:173
  503.7 5.5 reshape.306
  509.2 13.9 %multiply_reduce_fusion.3 = (f32[985,2]{1,0:T(8,128)}, f32[985,512]{1,0:T(8,128)}) fusion(f32[985,2,512]{2,1,0:T(2,128)} %reshape.306, f32[985,512]{1,0:T(8,128)} %reshape.308, f32[985,2]{1,0:T(8,128)} %copy.114), kind=kLoop, calls=%fused_computation.35 | loop fusion | flops 3528270 | bytes 8084880 | tf_op jit(solution)/shard_map/reduce_sum | solution.py:183
  527.0 3.2 fusion.30
  531.1 13.1 %fusion.9 = bf16[1,2048,512]{2,1,0:T(8,128)(2,1)} fusion(bf16[3456,2048]{1,0:T(8,128)(2,1)} %get-tuple-element.49, bf16[3456,512]{1,0:T(8,128)(2,1)} %bitcast.27), kind=kOutput, calls=%fused_computation.42 | convolution fusion | flops 7248805888 | bytes 19791872 | tf_op jit(solution)/shard_map/rh,rd->hd/dot_general | solution.py:203
  544.2 13.0 %fusion.10 = bf16[1,512,2048]{2,1,0:T(8,128)(2,1)} fusion(bf16[3456,512]{1,0:T(8,128)(2,1)} %bitcast.119, bf16[3456,2048]{1,0:T(8,128)(2,1)} %get-tuple-element.76), kind=kOutput, calls=%fused_computation.43 | convolution fusion | flops 7248805888 | bytes 19791872 | tf_op jit(solution)/shard_map/rd,rh->dh/dot_general | solution.py:207
  557.5 13.6 %all-to-all-done.2 = bf16[8,432,512]{2,1,0:T(8,128)(2,1)S(1)} async-done(((bf16[8,432,512]{2,1,0:T(8,128)(2,1)}), bf16[8,432,512]{2,1,0:T(8,128)(2,1)S(1)}, u32[]{:S(2)}, u32[]{:S(2)}) %all-to-all-start.2) | async-done | bytes 3538976 | tf_op jit(solution)/shard_map/all_to_all | solution.py:214
  571.2 9.2 %gather_fusion.1 = bf16[1970,512]{1,0:T(8,128)(2,1)} fusion(bf16[3456,512]{1,0:T(8,128)(2,1)S(1)} %bitcast.114, s32[2048]{0:T(1024)S(1)} %copy-done.51), kind=kCustom, calls=%fused_computation.1 | custom fusion | bytes 4042440 | tf_op jit(solution)/shard_map/gather | solution.py:216
  580.4 5.5 reshape.309
  585.9 8.4 %reduce_sum.274 = f32[985,512]{1,0:T(8,128)} reduce(f32[985,2,512]{2,1,0:T(2,128)} %reshape.309, f32[]{:T(128)} %constant.51.clone.1), dimensions={1}, to_apply=%region_15.17 | reduce | flops 504320 | bytes 6051844 | tf_op jit(solution)/shard_map/reduce_sum | solution.py:222
  594.3 4.7 multiply_reduce_fusion.6
  604.4 4.5 copy.119
  608.9 2.7 convolution_convert_fusion.7
  611.7 6.7 multiply_reduce_fusion.1
  618.4 4.7 multiply_convert_fusion.1
  627.7 2.9 fusion.52
  630.6 3.2 fusion.51
  633.8 4.1 copy.129
  637.9 4.0 reshape.300
  641.9 2.6 copy.126
  644.6 4.0 reshape.299
  651.2 4.0 reshape.298
  659.7 3.1 convolution_convert_fusion.2
  672.4 37.2 %pmax.7 = f32[8]{0:T(128)S(1)} all-reduce(f32[8]{0:T(128)S(1)} %get-tuple-element.18), channel_id=1, replica_groups=mesh['expert'=8,'fsdp'=4] {'expert','fsdp'}, use_global_device_ids=true, to_apply=%region_58.60 | all-reduce | flops 8 | bytes 64 | tf_op jit(solution)/shard_map/pmax | solution.py:339
  709.8 4.8 multiply_reduce_fusion.7
  718.2 6.4 all-reduce.10
  725.2 20.5 %all-reduce.8 = (bf16[128]{0:T(256)(128)(2,1)S(1)}, bf16[128]{0:T(256)(128)(2,1)S(1)}, bf16[128]{0:T(256)(128)(2,1)S(1)}, bf16[128]{0:T(256)(128)(2,1)S(1)}, bf1...) all-reduce(bf16[128]{0:T(256)(128)(2,1)S(1)} %dynamic-slice.1, ...), channel_id=1, replica_groups=mesh['expert'=8,'fsdp'=4] {'expert'}, use_global_device_ids=true, to_apply=%region_26.28 | all-reduce | flops 1920 | bytes 7680 | tf_op jit(solution)/shard_map/psum | solution.py:314
  752.2 38.5 %all-reduce.13.cloned.1.call-done = (bf16[128,1536]{1,0:T(8,128)(2,1)}, bf16[128,512]{1,0:T(8,128)(2,1)}) async-done(((bf16[128,1536]{1,0:T(8,128)(2,1)}, bf16[128,512]{1,0:T(8,128)(2,1)}), (bf16[128,1536]{1,0:T(8,128)(2,1)}, bf16[128,512]{1,0:T(8,128)(2,1)})) %all-reduce.13.cloned.1.call-update) | async-done | bytes 524304 | tf_op jit(solution)/shard_map/psum | solution.py:316
  (317 shorter events, 106.6 us)
Async XLA Ops:
  7.2 7.0 copy-start.66
  7.2 12.9 %copy-start.67 = (bf16[128]{0:T(256)(128)(2,1)S(1)}, bf16[128]{0:T(256)(128)(2,1)}, u32[]{:S(2)}) copy-start(bf16[128]{0:T(256)(128)(2,1)} %param.22) | copy-start | bytes 772
  7.2 18.3 %copy-start.68 = (bf16[128]{0:T(256)(128)(2,1)S(1)}, bf16[128]{0:T(256)(128)(2,1)}, u32[]{:S(2)}) copy-start(bf16[128]{0:T(256)(128)(2,1)} %param.24) | copy-start | bytes 772
  7.2 23.3 %copy-start.69 = (bf16[128]{0:T(256)(128)(2,1)S(1)}, bf16[128]{0:T(256)(128)(2,1)}, u32[]{:S(2)}) copy-start(bf16[128]{0:T(256)(128)(2,1)} %param.25) | copy-start | bytes 772
  7.3 28.3 %copy-start.70 = (bf16[128]{0:T(256)(128)(2,1)S(1)}, bf16[128]{0:T(256)(128)(2,1)}, u32[]{:S(2)}) copy-start(bf16[128]{0:T(256)(128)(2,1)} %param.27) | copy-start | bytes 772
  7.3 33.4 %copy-start.71 = (bf16[128]{0:T(256)(128)(2,1)S(1)}, bf16[128]{0:T(256)(128)(2,1)}, u32[]{:S(2)}) copy-start(bf16[128]{0:T(256)(128)(2,1)} %param.28) | copy-start | bytes 772
  7.3 38.4 %copy-start.72 = (bf16[128]{0:T(256)(128)(2,1)S(1)}, bf16[128]{0:T(256)(128)(2,1)}, u32[]{:S(2)}) copy-start(bf16[128]{0:T(256)(128)(2,1)} %param.29) | copy-start | bytes 772
  7.3 43.4 %copy-start.73 = (bf16[1,128]{1,0:T(2,128)(2,1)S(1)}, bf16[1,128]{1,0:T(2,128)(2,1)}, u32[]{:S(2)}) copy-start(bf16[1,128]{1,0:T(2,128)(2,1)} %param.34) | copy-start | bytes 772
  7.3 49.0 %copy-start.63 = (bf16[128,8]{0,1:T(8,128)(2,1)S(1)}, bf16[128,8]{0,1:T(8,128)(2,1)}, u32[]{:S(2)}) copy-start(bf16[128,8]{0,1:T(8,128)(2,1)} %param.30) | copy-start | bytes 6148
  7.3 54.2 %copy-start.64 = (bf16[1,512]{1,0:T(2,128)(2,1)S(1)}, bf16[1,512]{1,0:T(2,128)(2,1)}, u32[]{:S(2)}) copy-start(bf16[1,512]{1,0:T(2,128)(2,1)} %param.32) | copy-start | bytes 3076
  7.3 89.3 %all-gather.11.cloned.1.call-start = ((), (), s32[]{:S(2)}) async-start(), calls=%async_computation.10 | async-start | bytes 1966080 | tf_op jit(solution)/shard_map/all_gather | solution.py:76
  8.1 314.0 %all-gather.13.cloned.1.call-start = ((), (), s32[]{:S(2)}) async-start(), calls=%async_computation.11 | async-start | bytes 2621440 | tf_op jit(solution)/shard_map/all_gather | solution.py:84
  8.8 381.3 %all-gather.15.cloned.1.call-start = ((), (), s32[]{:S(2)}) async-start(), calls=%async_computation.12 | async-start | bytes 2621440 | tf_op jit(solution)/shard_map/all_gather | solution.py:86
  11.1 85.5 %copy-start.39 = (f32[985]{0:T(1024)}, f32[985]{0:T(1024)S(1)}, u32[]{:S(2)}) copy-start(f32[985]{0:T(1024)S(1)} %div.38) | copy-start | bytes 11824
  11.1 61.6 %copy-start.45 = (bf16[128,512]{1,0:T(8,128)(2,1)S(1)}, bf16[128,512]{1,0:T(8,128)(2,1)}, u32[]{:S(2)}) copy-start(bf16[128,512]{1,0:T(8,128)(2,1)} %param.26) | copy-start | bytes 393220
  14.2 122.7 %copy-start.5 = (f32[985,512]{1,0:T(8,128)}, f32[985,512]{1,0:T(8,128)S(1)}, u32[]{:S(2)}) copy-start(f32[985,512]{1,0:T(8,128)S(1)} %reshape.278) | copy-start | bytes 6051844
  20.2 76.5 %copy-start.46 = (f32[4,1,128]{2,1,0:T(1,128)}, f32[4,1,128]{2,1,0:T(1,128)S(1)}, u32[]{:S(2)}) copy-start(f32[4,1,128]{2,1,0:T(1,128)S(1)} %convert_element_type.334) | copy-start | bytes 6148
  25.5 71.1 %copy-start.55 = (f32[4,1,128]{2,1,0:T(1,128)}, f32[4,1,128]{2,1,0:T(1,128)S(1)}, u32[]{:S(2)}) copy-start(f32[4,1,128]{2,1,0:T(1,128)S(1)} %convert_element_type.335) | copy-start | bytes 6148
  45.7 94.3 %copy-start.52 = (f32[4,1,128]{2,1,0:T(1,128)}, f32[4,1,128]{2,1,0:T(1,128)S(1)}, u32[]{:S(2)}) copy-start(f32[4,1,128]{2,1,0:T(1,128)S(1)} %convert_element_type.339) | copy-start | bytes 6148
  50.7 89.3 %copy-start.61 = (f32[4,1,128]{2,1,0:T(1,128)}, f32[4,1,128]{2,1,0:T(1,128)S(1)}, u32[]{:S(2)}) copy-start(f32[4,1,128]{2,1,0:T(1,128)S(1)} %convert_element_type.340) | copy-start | bytes 6148
  61.5 78.5 %copy-start.48 = (bf16[512,8]{0,1:T(8,128)(2,1)}, bf16[512,8]{0,1:T(8,128)(2,1)S(1)}, u32[]{:S(2)}) copy-start(bf16[512,8]{0,1:T(8,128)(2,1)S(1)} %all_gather.51) | copy-start | bytes 24580
  67.3 29.3 %copy-start.41 = (f32[985]{0:T(1024)}, f32[985]{0:T(1024)S(1)}, u32[]{:S(2)}) copy-start(f32[985]{0:T(1024)S(1)} %rsqrt.20) | copy-start | bytes 11824
  72.2 73.3 %copy-start.60 = (s32[1970,1]{0,1:T(1,128)}, s32[1970,1]{0,1:T(1,128)S(1)}, u32[]{:S(2)}) copy-start(s32[1970,1]{0,1:T(1,128)S(1)} %compare_select_fusion) | copy-start | bytes 23644
  114.4 11.1 %copy-start.11 = (bf16[5,197,8,64]{1,3,2,0:T(8,128)(2,1)}, bf16[5,197,8,64]{1,3,2,0:T(8,128)(2,1)S(1)}, u32[]{:S(2)}) copy-start(bf16[5,197,8,64]{1,3,2,0:T(8,128)(2,1)S(1)} %copy.110) | copy-start | bytes 3025924
  142.4 26.7 %copy-start.54 = (f32[985]{0:T(1024)}, f32[985]{0:T(1024)S(1)}, u32[]{:S(2)}) copy-start(f32[985]{0:T(1024)S(1)} %get-tuple-element.66) | copy-start | bytes 11824
  162.1 7.0 copy-start.34
  163.8 57.0 %collective-permute-start.2 = (bf16[1,432,512]{2,1,0:T(8,128)(2,1)}, bf16[1,432,512]{2,1,0:T(8,128)(2,1)}, u32[]{:S(2)}, u32[]{:S(2)}) collective-permute-start(bf16[1,432,512]{2,1,0:T(8,128)(2,1)} %get-tuple-element.57), channel_id=1, source_target_pairs={{0,20},{4,24},{8,28},{12,0},{16,4},{20,8},{24,12},{28,16},{1,21},{... | collective-permute-start | bytes 1327112 | tf_op jit(solution)/shard_map/ppermute | solution.py:20
  167.2 52.4 %collective-permute-start.1 = (bf16[1,432,512]{2,1,0:T(8,128)(2,1)}, bf16[1,432,512]{2,1,0:T(8,128)(2,1)}, u32[]{:S(2)}, u32[]{:S(2)}) collective-permute-start(bf16[1,432,512]{2,1,0:T(8,128)(2,1)} %get-tuple-element.58), channel_id=1, source_target_pairs={{0,24},{4,28},{8,0},{12,4},{16,8},{20,12},{24,16},{28,20},{1,25},{... | collective-permute-start | bytes 1327112 | tf_op jit(solution)/shard_map/ppermute | solution.py:20
  168.6 30.8 %collective-permute-start = (bf16[1,432,512]{2,1,0:T(8,128)(2,1)}, bf16[1,432,512]{2,1,0:T(8,128)(2,1)}, u32[]{:S(2)}, u32[]{:S(2)}) collective-permute-start(bf16[1,432,512]{2,1,0:T(8,128)(2,1)} %get-tuple-element.59), channel_id=1, source_target_pairs={{0,28},{4,0},{8,4},{12,8},{16,12},{20,16},{24,20},{28,24},{1,29},{... | collective-permute-start | bytes 1327112 | tf_op jit(solution)/shard_map/ppermute | solution.py:20
  169.7 66.2 %collective-permute-start.3 = (bf16[1,432,512]{2,1,0:T(8,128)(2,1)}, bf16[1,432,512]{2,1,0:T(8,128)(2,1)}, u32[]{:S(2)}, u32[]{:S(2)}) collective-permute-start(bf16[1,432,512]{2,1,0:T(8,128)(2,1)} %get-tuple-element.56), channel_id=1, source_target_pairs={{0,16},{4,20},{8,24},{12,28},{16,0},{20,4},{24,8},{28,12},{1,17},{... | collective-permute-start | bytes 1327112 | tf_op jit(solution)/shard_map/ppermute | solution.py:20
  193.0 209.6 %all-to-all-start.1 = ((bf16[8,432,512]{2,1,0:T(8,128)(2,1)}), bf16[8,432,512]{2,1,0:T(8,128)(2,1)}, u32[]{:S(2)}, u32[]{:S(2)}) async-start(bf16[8,432,512]{2,1,0:T(8,128)(2,1)} %bitcast.116), calls=%async_computation.1 | async-start | bytes 7077888 | tf_op jit(solution)/shard_map/all_to_all | solution.py:195
  197.5 123.2 %collective-permute-start.6 = (bf16[1,432,512]{2,1,0:T(8,128)(2,1)}, bf16[1,432,512]{2,1,0:T(8,128)(2,1)S(1)}, u32[]{:S(2)}, u32[]{:S(2)}) collective-permute-start(bf16[1,432,512]{2,1,0:T(8,128)(2,1)} %get-tuple-element.53), channel_id=1, source_target_pairs={{0,4},{4,8},{8,12},{12,16},{16,20},{20,24},{24,28},{28,0},{1,5},{5... | collective-permute-start | bytes 1327112 | tf_op jit(solution)/shard_map/ppermute | solution.py:20
  199.4 121.2 %collective-permute-start.4 = (bf16[1,432,512]{2,1,0:T(8,128)(2,1)}, bf16[1,432,512]{2,1,0:T(8,128)(2,1)S(1)}, u32[]{:S(2)}, u32[]{:S(2)}) collective-permute-start(bf16[1,432,512]{2,1,0:T(8,128)(2,1)} %get-tuple-element.55), channel_id=1, source_target_pairs={{0,12},{4,16},{8,20},{12,24},{16,28},{20,0},{24,4},{28,8},{1,13},{... | collective-permute-start | bytes 1327112 | tf_op jit(solution)/shard_map/ppermute | solution.py:20
  219.5 101.1 %collective-permute-start.5 = (bf16[1,432,512]{2,1,0:T(8,128)(2,1)}, bf16[1,432,512]{2,1,0:T(8,128)(2,1)S(1)}, u32[]{:S(2)}, u32[]{:S(2)}) collective-permute-start(bf16[1,432,512]{2,1,0:T(8,128)(2,1)} %get-tuple-element.54), channel_id=1, source_target_pairs={{0,8},{4,12},{8,16},{12,20},{16,24},{20,28},{24,0},{28,4},{1,9},{5... | collective-permute-start | bytes 1327112 | tf_op jit(solution)/shard_map/ppermute | solution.py:20
  322.0 68.0 %copy-start.26 = (bf16[8,432,512]{2,1,0:T(8,128)(2,1)}, bf16[8,432,512]{2,1,0:T(8,128)(2,1)S(1)}, u32[]{:S(2)}) copy-start(bf16[8,432,512]{2,1,0:T(8,128)(2,1)S(1)} %fusion.7) | copy-start | bytes 10616836
  322.1 68.0 %copy-start.65 = (f32[1,512]{1,0:T(1,128)S(1)}, f32[1,512]{1,0:T(1,128)}, u32[]{:S(2)}) copy-start(f32[1,512]{1,0:T(1,128)} %add.224) | copy-start | bytes 6148
  402.6 83.8 %all-to-all-start = ((bf16[8,432,512]{2,1,0:T(8,128)(2,1)}), bf16[8,432,512]{2,1,0:T(8,128)(2,1)S(1)}, u32[]{:S(2)}, u32[]{:S(2)}) async-start(bf16[8,432,512]{2,1,0:T(8,128)(2,1)} %bitcast.121), calls=%async_computation | async-start | bytes 7077888 | tf_op jit(solution)/shard_map/all_to_all | solution.py:171
  407.2 257.0 %reduce-scatter.26.cloned.1.call-start = ((), (), s32[]{:S(2)}) async-start(), calls=%async_computation.19 | async-start | bytes 163840
  410.6 255.0 %reduce-scatter.24.cloned.1.call-start = ((), (), s32[]{:S(2)}) async-start(), calls=%async_computation.18 | async-start | bytes 655360
  488.2 83.0 %all-to-all-start.2 = ((bf16[8,432,512]{2,1,0:T(8,128)(2,1)}), bf16[8,432,512]{2,1,0:T(8,128)(2,1)S(1)}, u32[]{:S(2)}, u32[]{:S(2)}) async-start(bf16[8,432,512]{2,1,0:T(8,128)(2,1)} %bitcast.120), calls=%async_computation.2 | async-start | bytes 7077888 | tf_op jit(solution)/shard_map/all_to_all | solution.py:214
  491.9 175.3 %reduce-scatter.22.cloned.1.call-start = ((), (), s32[]{:S(2)}) async-start(), calls=%async_computation.17 | async-start | bytes 163840
  509.2 15.7 %copy-start.44 = (s32[985,2]{0,1:T(2,128)S(1)}, s32[985,2]{0,1:T(2,128)}, u32[]{:S(2)}) copy-start(s32[985,2]{0,1:T(2,128)} %param.35) | copy-start | bytes 23644
  509.2 17.8 %copy-start.36 = (f32[985]{0:T(1024)S(1)}, f32[985]{0:T(1024)}, u32[]{:S(2)}) copy-start(f32[985]{0:T(1024)} %copy-done.35) | copy-start | bytes 11824
  509.2 17.8 %copy-start.38 = (f32[985]{0:T(1024)S(1)}, f32[985]{0:T(1024)}, u32[]{:S(2)}) copy-start(f32[985]{0:T(1024)} %copy-done.37) | copy-start | bytes 11824
  531.0 137.0 %reduce-scatter.20.cloned.1.call-start = ((), (), s32[]{:S(2)}) async-start(), calls=%async_computation.16 | async-start | bytes 2621440 | tf_op jit(solution)/shard_map/reduce_scatter | solution.py:332
  544.2 27.0 %copy-start.51 = (s32[2048]{0:T(1024)S(1)}, s32[2048]{0:T(1024)}, u32[]{:S(2)}) copy-start(s32[2048]{0:T(1024)} %pad_clamp_fusion) | copy-start | bytes 24580
  544.2 126.1 %reduce-scatter.18.cloned.1.call-start = ((), (), s32[]{:S(2)}) async-start(), calls=%async_computation.15 | async-start | bytes 2621440 | tf_op jit(solution)/shard_map/reduce_scatter | solution.py:326
  557.3 159.5 %reduce-scatter.16.cloned.1.call-start = ((), (), s32[]{:S(2)}) async-start(), calls=%async_computation.14 | async-start | bytes 655360 | tf_op jit(solution)/shard_map/reduce_scatter | solution.py:297
  585.8 8.4 %copy-start.3 = (f32[985,512]{1,0:T(8,128)S(1)}, f32[985,512]{1,0:T(8,128)}, u32[]{:S(2)}) copy-start(f32[985,512]{1,0:T(8,128)} %copy-done.2) | copy-start | bytes 6051844
  585.8 8.4 %copy-start.31 = (f32[985,8]{0,1:T(8,128)S(1)}, f32[985,8]{0,1:T(8,128)}, u32[]{:S(2)}) copy-start(f32[985,8]{0,1:T(8,128)} %copy-done.30) | copy-start | bytes 94564
  585.8 8.4 %copy-start.33 = (f32[985,8]{0,1:T(8,128)S(1)}, f32[985,8]{0,1:T(8,128)}, u32[]{:S(2)}) copy-start(f32[985,8]{0,1:T(8,128)} %copy-done.32) | copy-start | bytes 94564
  585.8 8.4 %copy-start.49 = (bf16[512,8]{0,1:T(8,128)(2,1)S(1)}, bf16[512,8]{0,1:T(8,128)(2,1)}, u32[]{:S(2)}) copy-start(bf16[512,8]{0,1:T(8,128)(2,1)} %copy-done.48) | copy-start | bytes 24580
  585.8 8.4 %copy-start.53 = (f32[4,1,128]{2,1,0:T(1,128)S(1)}, f32[4,1,128]{2,1,0:T(1,128)}, u32[]{:S(2)}) copy-start(f32[4,1,128]{2,1,0:T(1,128)} %copy-done.52) | copy-start | bytes 6148
  585.8 8.4 %copy-start.58 = (f32[985]{0:T(1024)S(1)}, f32[985]{0:T(1024)}, u32[]{:S(2)}) copy-start(f32[985]{0:T(1024)} %copy-done.57) | copy-start | bytes 11824
  604.4 7.3 copy-start.14
  604.4 7.3 copy-start.29
  611.7 16.0 %slice-start = ((s8[8192000]{0:T(1024)(128)(4,1)}), s8[4194304]{0:T(1024)(128)(4,1)S(1)}, s32[]{:S(2)}) async-start(s8[8192000]{0:T(1024)(128)(4,1)} %bitcast.112), calls=%async_computation.21 | async-start | bytes 8388608
  618.4 9.2 %slice-start.1 = ((s8[8192000]{0:T(1024)(128)(4,1)}), s8[3997696]{0:T(1024)(128)(4,1)S(1)}, s32[]{:S(2)}) async-start(s8[8192000]{0:T(1024)(128)(4,1)} %bitcast.112), calls=%async_computation.22 | async-start | bytes 7995392
  630.5 86.2 %reduce-scatter.14.cloned.1.call-start = ((), (), s32[]{:S(2)}) async-start(), calls=%async_computation.13 | async-start | bytes 1966080 | tf_op jit(solution)/shard_map/reduce_scatter | solution.py:288
  633.8 8.1 %copy-start.21 = (bf16[5,197,8,64]{1,3,2,0:T(8,128)(2,1)S(1)}, bf16[5,197,8,64]{1,3,2,0:T(8,128)(2,1)}, u32[]{:S(2)}) copy-start(bf16[5,197,8,64]{1,3,2,0:T(8,128)(2,1)} %fusion.27) | copy-start | bytes 3025924
  662.8 46.8 %copy-start.74 = (s32[8]{0:T(128)S(1)}, s32[8]{0:T(128)}, u32[]{:S(2)}) copy-start(s32[8]{0:T(128)} %param.36) | copy-start | bytes 100
  662.8 127.8 %all-reduce.13.cloned.1.call-start = ((), (), s32[]{:S(2)}) async-start(), calls=%async_computation.20 | async-start | bytes 1048576 | tf_op jit(solution)/shard_map/psum | solution.py:316
  716.7 33.1 %copy-start.19 = (f32[985,512]{1,0:T(8,128)S(1)}, f32[985,512]{1,0:T(8,128)}, u32[]{:S(2)}) copy-start(f32[985,512]{1,0:T(8,128)} %multiply_add_fusion) | copy-start | bytes 6051844
  716.7 34.7 %copy-start.27 = (bf16[128,1536]{1,0:T(8,128)(2,1)S(1)}, bf16[128,1536]{1,0:T(8,128)(2,1)}, u32[]{:S(2)}) copy-start(bf16[128,1536]{1,0:T(8,128)(2,1)} %param.23) | copy-start | bytes 1179652
  (35 other events, 117.6 us)
Sparse Core Ops, SparseCore 0:
  9.7 22.3 all-gather.10
  33.7 22.6 all-gather.12
  57.9 24.8 all-gather.14
  410.7 20.0 reduce-scatter.25
  444.3 22.0 reduce-scatter.23
  531.2 19.9 reduce-scatter.21
  553.9 31.3 reduce-scatter.19
  587.8 31.4 reduce-scatter.17
  630.7 19.5 reduce-scatter.15
  663.0 26.2 reduce-scatter.13
  716.9 73.7 all-reduce.12
